TPU v7x, 128 devices: a whole 4x4x4 slice. The times are simulated.
128 devices in a mesh: dp: 8 (over x, core), fsdp: 16 (over z, y).
Axes of the slice: x: 4, y: 4, z: 4, core: 2. Of those that a mesh axis runs over, the one named last changes fastest.
Arguments:
- tokens: bfloat16 [65536, 1408], P(('dp', 'fsdp')), may hold values from -6 to 6
- image_of: int32 [65536], P(('dp', 'fsdp')), may hold values from 0 to 16383, as said below
- live: int32 [65536], P(('dp', 'fsdp')), may hold values from 0 to 1, as said below
- request_of: int32 [16384], P('dp'), may hold values from -1 to 63, as said below
- ln1_gain: float32 [1408], replicated, may hold values from 0.5 to 1.5
- ln1_shift: float32 [1408], replicated, may hold values from -3 to 3
- w_qkv: bfloat16 [1408, 4224], P('fsdp')
- b_qkv: float32 [4224], replicated, may hold values from -3 to 3
- w_out: bfloat16 [1408, 1408], P('fsdp'), may hold values from -0.15625 to 0.15625
- b_out: float32 [1408], replicated, may hold values from -3 to 3
- ln2_gain: float32 [1408], replicated, may hold values from 0.5 to 1.5
- ln2_shift: float32 [1408], replicated, may hold values from -3 to 3
- w_proj: bfloat16 [5632, 4096], P(None, 'fsdp'), may hold values from -0.078125 to 0.078125
- b_proj: float32 [4096], P('fsdp'), may hold values from -3 to 3
Outputs:
- features: bfloat16 [16384, 4096], P('dp', 'fsdp')
- peaks: float32 [64], replicated
Inputs may be any that keep to these rules, and one draw needn't show every extreme that they name: `image_of`: tokens come in aligned groups of 4 of one image; an image's tokens are consecutive and lie within one aligned block of 512 rows; numbers never fall along the rows; the last block's last group of 4 is an image of its own. Padding fills whole groups of 4 at the end of each aligned block of 512 rows, at most half of the block; the first group of every block is live and the last block has none; a padding token carries the image number of the token before it. `request_of`: -1 exactly on merged rows of padding; on the other rows request numbers never fall along the rows, and every request has some row.
All inputs are finite; a program needn't handle non-finite values.
Results may differ from a plain program's by a relative error of at most 0.012.
The roundings to bfloat16 on the way count: a program that leaves them out, or rounds other values in their place, can miss the bound.
Values may be sent and summed in bfloat16 or wider, within the bound.
A program may use at most 192 MiB of HBM per device.

v0:
```python
import jax
import jax.numpy as jnp
from jax import lax
from jax.sharding import PartitionSpec as P

HEADS = 16


def normalize(values, gain, shift):
    mean_value = jnp.mean(values, axis=-1, keepdims=True)
    centred = values - mean_value
    variance = jnp.mean(centred * centred, axis=-1, keepdims=True)
    return centred * lax.rsqrt(variance + 1e-06) * gain + shift


def attention(qkv, image_ids, live_flags, heads):
    count_rows = qkv.shape[0]
    width = qkv.shape[1] // 3
    head_size = width // heads
    scale = head_size ** (-0.5)
    queries = qkv[:, :width].reshape(count_rows, heads, head_size)
    keys_all = qkv[:, width : 2 * width].reshape(count_rows, heads, head_size)
    values_all = qkv[:, 2 * width :].reshape(count_rows, heads, head_size)
    block_rows = min(512, count_rows)
    blocks = count_rows // block_rows
    key_live = live_flags[None, :] == 1

    def one_block(items):
        block_queries, block_images = items
        scores = (
            jnp.einsum("qhe,khe->hqk", block_queries, keys_all, preferred_element_type=jnp.float32)
            * scale
        )
        allowed = (block_images[:, None] == image_ids[None, :]) & key_live
        scores = jnp.where(allowed[None], scores, jnp.float32(-1e30))
        top = jnp.max(scores, axis=-1, keepdims=True)
        expo = jnp.exp(scores - top)
        weights = (expo / jnp.sum(expo, axis=-1, keepdims=True)).astype(jnp.bfloat16)
        mixed = jnp.einsum("hqk,khe->qhe", weights, values_all, preferred_element_type=jnp.float32)
        return mixed.reshape(block_rows, width).astype(jnp.bfloat16)

    result = lax.map(
        one_block,
        (
            queries.reshape(blocks, block_rows, heads, head_size),
            image_ids.reshape(blocks, block_rows),
        ),
    )
    return result.reshape(count_rows, width)


def shards(
    tokens,
    image_of,
    live,
    request_of,
    ln1_gain,
    ln1_shift,
    w_qkv,
    b_qkv,
    w_out,
    b_out,
    ln2_gain,
    ln2_shift,
    w_proj,
    b_proj,
):
    count_rows = tokens.shape[0]
    width = tokens.shape[1]
    resid = tokens.astype(jnp.float32)
    normed = normalize(resid, ln1_gain, ln1_shift).astype(jnp.bfloat16)
    columns = normed
    mixed = jnp.dot(
        columns,
        lax.all_gather(w_qkv, "fsdp", axis=0, tiled=True),
        preferred_element_type=jnp.float32,
    )
    qkv = (mixed + b_qkv).astype(jnp.bfloat16)
    attended = attention(qkv, image_of, live, HEADS)
    columns = attended
    projected_out = jnp.dot(
        columns,
        lax.all_gather(w_out, "fsdp", axis=0, tiled=True),
        preferred_element_type=jnp.float32,
    )
    resid = resid + (projected_out + b_out)
    normed2 = normalize(resid, ln2_gain, ln2_shift).astype(jnp.bfloat16)
    merged = normed2.reshape(count_rows // 4, 4 * width)
    projected = (
        jnp.dot(
            lax.all_gather(merged, "fsdp", axis=0, tiled=True),
            w_proj,
            preferred_element_type=jnp.float32,
        )
        + b_proj
    )
    requests = lax.axis_size("dp") * lax.axis_size("fsdp") // 2
    columns_here = projected.shape[1]
    labels = jnp.arange(requests, dtype=jnp.int32)
    member = request_of[:, None] == labels[None, :]
    row_squares = jnp.sum(projected * projected, axis=1)
    row_top = jnp.max(projected, axis=1)
    sums_part = jnp.sum(jnp.where(member, row_squares[:, None], jnp.float32(0.0)), axis=0)
    entries_part = jnp.sum(member.astype(jnp.float32), axis=0) * jnp.float32(columns_here)
    top_part = jnp.max(jnp.where(member, row_top[:, None], jnp.float32(-jnp.inf)), axis=0)
    sumsq, entries = lax.psum((sums_part, entries_part), ("dp", "fsdp"))
    top = lax.pmax(top_part, ("dp", "fsdp"))
    rms = jnp.sqrt(sumsq / entries + 1e-06)
    valid = request_of >= 0
    row_rms = jnp.sum(jnp.where(member, rms[None, :], jnp.float32(0.0)), axis=1) + jnp.where(
        valid, 0.0, 1.0
    )
    features = jnp.where(valid[:, None], projected / row_rms[:, None], jnp.float32(0.0)).astype(
        jnp.bfloat16
    )
    peaks = top / rms
    return (features, peaks)


def solution(mesh):
    return jax.shard_map(
        shards,
        mesh=mesh,
        in_specs=(
            P(("dp", "fsdp"), None),
            P(("dp", "fsdp")),
            P(("dp", "fsdp")),
            P("dp"),
            P(),
            P(),
            P("fsdp", None),
            P(),
            P("fsdp", None),
            P(),
            P(),
            P(),
            P(None, "fsdp"),
            P("fsdp"),
        ),
        out_specs=(P("dp", "fsdp"), P()),
        check_vma=False,
    )
```

profile of v0, /device:TPU:1, one launch (start us, length us, event | category | flops | bytes accessed | tf_op | source)
XLA Modules:
  0.0 461.9 jit_solution(2938531197813447947)
XLA Ops:
  7.3 0.7 all-gather.4.cloned.1.call-update
  8.0 0.7 all-gather.6.cloned.1.call-update
  8.8 1.6 convert_reduce_fusion
  10.4 1.9 fusion.8
  12.6 87.9 %all-gather.4.cloned.1.call-done = bf16[1408,4224]{1,0:T(8,128)(2,1)} async-done(((bf16[88,4224]{1,0:T(8,128)(2,1)}), bf16[1408,4224]{1,0:T(8,128)(2,1)}) %all-gather.4.cloned.1.call-update) | async-done | bytes 11894800 | tf_op jit(solution)/shard_map/all_gather | solution.py:75
  100.5 12.4 %add_convert_fusion = bf16[512,4224]{1,0:T(8,128)(2,1)S(1)} fusion(bf16[1408,4224]{1,0:T(8,128)(2,1)} %all-gather.4.cloned.1.call-done, f32[4224]{0:T(1024)S(1)} %copy-done.7, bf16[512,1408]{1,0:T(8,128)(2,1)} %param.14, f32[1408]{0:T(1024)S(1)} %copy-done.8, f32[1408]{0:T(1024)S(1)} %copy-done.9, f32[512]{0:T(512)S(1)} %add_rsqrt_fusion.1, ...), kind=kOutput, calls=%fused_computation.5 | convolution fusion | flops 6098780160 | bytes 17694208 | tf_op jit(solution)/shard_map/dot_general | solution.py:73
  112.8 2.1 fusion.23
  115.0 2.6 copy.27
  117.6 2.5 copy.28
  120.1 2.6 copy.26
  122.7 11.0 %fusion.24 = (f32[16,512]{1,0:T(8,128)S(1)}, f32[16,512,512]{1,2,0:T(8,128)}) fusion(pred[512,512]{0,1:T(8,128)(4,1)S(1)} %compare_and_fusion, bf16[512,16,88]{0,2,1:T(8,128)(2,1)} %bitcast.17, bf16[512,16,88]{0,2,1:T(8,128)(2,1)} %bitcast.18), kind=kOutput, calls=%fused_computation.50 | convolution fusion | flops 754975232 | bytes 19955712 | tf_op jit(solution)/shard_map/while/body/eval_jaxpr/sub | solution.py:37
  133.7 8.9 %fusion.14 = bf16[16,88,512]{2,1,0:T(8,128)(2,1)} fusion(bf16[512,16,88]{0,2,1:T(8,128)(2,1)} %bitcast.19, f32[16,512,512]{1,2,0:T(8,128)} %get-tuple-element.46, f32[16,512]{1,0:T(8,128)S(1)} %get-tuple-element.45), kind=kOutput, calls=%fused_computation.26 | convolution fusion | flops 747307008 | bytes 19693568 | tf_op jit(solution)/shard_map/while/body/eval_jaxpr/hqk,khe->qhe/dot_general | solution.py:39
  142.5 10.3 %all-gather.6.cloned.1.call-done = bf16[1408,1408]{1,0:T(8,128)(2,1)} async-done(((bf16[88,1408]{1,0:T(8,128)(2,1)}), bf16[1408,1408]{1,0:T(8,128)(2,1)}) %all-gather.6.cloned.1.call-update) | async-done | bytes 3964944 | tf_op jit(solution)/shard_map/all_gather | solution.py:83
  152.9 5.9 %fusion.25 = (f32[512]{0:T(512)S(1)}, f32[512,1408]{1,0:T(8,128)S(1)}) fusion(f32[1408]{0:T(1024)S(1)} %copy-done.2, bf16[512,1408]{0,1:T(8,128)(2,1)} %bitcast.16, bf16[1408,1408]{1,0:T(8,128)(2,1)} %all-gather.6.cloned.1.call-done, bf16[512,1408]{1,0:T(8,128)(2,1)} %param.14), kind=kOutput, calls=%fused_computation.51 | convolution fusion | flops 2032926208 | bytes 9739776 | tf_op jit(solution)/shard_map/dot_general | solution.py:81
  158.8 0.4 multiply_reduce_fusion
  159.5 1.7 add_convert_fusion.1
  161.2 3.6 reshape.109
  164.8 143.3 %all-gather.8.cloned.1.call-done = bf16[2048,5632]{1,0:T(8,128)(2,1)} async-done(((bf16[128,5632]{1,0:T(8,128)(2,1)}), bf16[2048,5632]{1,0:T(8,128)(2,1)}) %all-gather.8.cloned.1.call-update) | async-done | bytes 23068688 | tf_op jit(solution)/shard_map/all_gather | solution.py:91
  308.2 12.5 %fusion.22 = (f32[2048]{0:T(1024)S(1)}, f32[2048]{0:T(1024)S(1)}, f32[2048,256]{0,1:T(8,128)}) fusion(f32[256]{0:T(256)S(1)} %copy-done.10, bf16[2048,5632]{1,0:T(8,128)(2,1)} %all-gather.8.cloned.1.call-done, bf16[5632,256]{1,0:T(8,128)(2,1)S(1)} %copy-done), kind=kOutput, calls=%fused_computation.48 | convolution fusion | flops 5907673088 | bytes 28066816 | tf_op jit(solution)/shard_map/dot_general | solution.py:90
  320.9 64.6 %all-reduce = (f32[64]{0:T(128)S(1)}, f32[64]{0:T(128)S(1)}) all-reduce(f32[64]{0:T(128)S(1)} %get-tuple-element.37, f32[64]{0:T(128)S(1)} %broadcast_multiply_fusion.2), channel_id=1, replica_groups=mesh['dp'=8,'fsdp'=16] {'dp','fsdp'}, use_global_device_ids=true, to_apply=%region_8.9 | all-reduce | flops 128 | bytes 1024 | tf_op jit(solution)/shard_map/psum | solution.py:106
  385.7 64.1 %pmax.7 = f32[64]{0:T(128)S(1)} all-reduce(f32[64]{0:T(128)S(1)} %get-tuple-element.34), channel_id=1, replica_groups=mesh['dp'=8,'fsdp'=16] {'dp','fsdp'}, use_global_device_ids=true, to_apply=%region_14.15 | all-reduce | flops 64 | bytes 512 | tf_op jit(solution)/shard_map/pmax | solution.py:107
  449.8 0.5 div.47
  450.3 2.8 select_convert_fusion
  453.2 2.3 copy.30
  (37 shorter events, 1.1 us)
Async XLA Ops:
  7.2 301.0 %copy-start = (bf16[5632,256]{1,0:T(8,128)(2,1)S(1)}, bf16[5632,256]{1,0:T(8,128)(2,1)}, u32[]{:S(2)}) copy-start(bf16[5632,256]{1,0:T(8,128)(2,1)} %param.26) | copy-start | bytes 8650756
  7.2 5.1 %copy-start.6 = (s32[512]{0:T(512)S(1)}, s32[512]{0:T(512)}, u32[]{:S(2)}) copy-start(s32[512]{0:T(512)} %param.16) | copy-start | bytes 6148
  7.2 5.1 %copy-start.5 = (s32[512]{0:T(512)S(1)}, s32[512]{0:T(512)}, u32[]{:S(2)}) copy-start(s32[512]{0:T(512)} %param.15) | copy-start | bytes 6148
  7.2 93.3 %copy-start.9 = (f32[1408]{0:T(1024)S(1)}, f32[1408]{0:T(1024)}, u32[]{:S(2)}) copy-start(f32[1408]{0:T(1024)} %param.18) | copy-start | bytes 16900
  7.2 93.3 %copy-start.8 = (f32[1408]{0:T(1024)S(1)}, f32[1408]{0:T(1024)}, u32[]{:S(2)}) copy-start(f32[1408]{0:T(1024)} %param.19) | copy-start | bytes 16900
  7.2 93.3 %copy-start.7 = (f32[4224]{0:T(1024)S(1)}, f32[4224]{0:T(1024)}, u32[]{:S(2)}) copy-start(f32[4224]{0:T(1024)} %param.21) | copy-start | bytes 50692
  7.2 93.2 %all-gather.4.cloned.1.call-start = ((), (), s32[]{:S(2)}) async-start(), calls=%async_computation | async-start | bytes 12638208 | tf_op jit(solution)/shard_map/all_gather | solution.py:75
  8.0 144.9 %all-gather.6.cloned.1.call-start = ((), (), s32[]{:S(2)}) async-start(), calls=%async_computation.1 | async-start | bytes 4212736 | tf_op jit(solution)/shard_map/all_gather | solution.py:83
  8.7 299.4 %all-gather.8.cloned.1.call-start = ((), (), s32[]{:S(2)}) async-start(), calls=%async_computation.2 | async-start | bytes 24510464 | tf_op jit(solution)/shard_map/all_gather | solution.py:91
  133.7 19.2 %copy-start.2 = (f32[1408]{0:T(1024)S(1)}, f32[1408]{0:T(1024)}, u32[]{:S(2)}) copy-start(f32[1408]{0:T(1024)} %param.23) | copy-start | bytes 16900
  158.8 0.7 copy-start.3
  158.8 0.7 copy-start.4
  161.2 147.0 %copy-start.10 = (f32[256]{0:T(256)S(1)}, f32[256]{0:T(256)}, u32[]{:S(2)}) copy-start(f32[256]{0:T(256)} %param.27) | copy-start | bytes 3076
  164.8 155.8 %copy-start.1 = (s32[2048]{0:T(1024)S(1)}, s32[2048]{0:T(1024)}, u32[]{:S(2)}) copy-start(s32[2048]{0:T(1024)} %param.17) | copy-start | bytes 24580
Sparse Core Ops, SparseCore 0:
  10.2 90.2 all-gather.3
  102.6 50.2 all-gather.5
  164.9 143.1 all-gather.7
where the time goes:
time: 462 us
  waiting for transfers between devices  243 us (53%)
  blocking collectives  129 us (28%)
  matrix products  50.6 us (11%)
  local copies, waits for them, and re-layouts  16 us (3%)
  between operations  13.9 us (3%)
  other arithmetic  9.62 us (2%)
    all_gather x1, waiting for transfers between devices, shards(): lax.all_gather(merged, 'fsdp', axis=0, tiled=True)  143 us
    all_gather x1, waiting for transfers between devices, shards(): lax.all_gather(w_qkv, 'fsdp', axis=0, tiled=True)  87.9 us
    psum x1, blocking collectives, shards(): sumsq, entries = lax.psum((sums_part, entries_part), ('dp', 'fsdp'))  64.6 us
    pmax x1, blocking collectives, shards(): top = lax.pmax(top_part, ('dp', 'fsdp'))  64.1 us
    dot_general x1, matrix products, shards(): jnp.dot(lax.all_gather(merged, 'fsdp', axis=0, tiled=True), w_proj, prefe...  12.5 us
    dot_general x1, matrix products, shards(): jnp.dot(columns, lax.all_gather(w_qkv, 'fsdp', axis=0, tiled=True), prefe...  12.4 us
    sub x1, matrix products, one_block(): expo = jnp.exp(scores - top)  11 us
    all_gather x1, waiting for transfers between devices, shards(): lax.all_gather(w_out, 'fsdp', axis=0, tiled=True)  10.3 us
  transfers between devices with their start and end apart: 3, of which 3 were waited for; matrix products, arithmetic and copies ran while one was open for 10% of the time, Pallas kernels for 0%

commit v1 on v0

--- a/solution.py
+++ b/solution.py
@@ -4,6 +4,11 @@
 from jax.sharding import PartitionSpec as P
 
 HEADS = 16
+
+
+def one_after_other(value, inner_axis, outer_axis):
+    partial = lax.psum(value, inner_axis)
+    return lax.psum(partial, outer_axis)
 
 
 def normalize(values, gain, shift):
@@ -103,7 +108,7 @@
     sums_part = jnp.sum(jnp.where(member, row_squares[:, None], jnp.float32(0.0)), axis=0)
     entries_part = jnp.sum(member.astype(jnp.float32), axis=0) * jnp.float32(columns_here)
     top_part = jnp.max(jnp.where(member, row_top[:, None], jnp.float32(-jnp.inf)), axis=0)
-    sumsq, entries = lax.psum((sums_part, entries_part), ("dp", "fsdp"))
+    sumsq, entries = one_after_other((sums_part, entries_part), "fsdp", "dp")
     top = lax.pmax(top_part, ("dp", "fsdp"))
     rms = jnp.sqrt(sumsq / entries + 1e-06)
     valid = request_of >= 0

time: 462 us -> 447 us (0.968)
  blocking collectives: 129 us -> 113 us
    psum x1 -> x2, blocking collectives: 64.6 us -> 50.9 us  [the longest x1 31.6 us: one_after_other(): partial = lax.psum(value, inner_axis)]
where the time goes in v1:
time: 447 us; the launch traced here: 446 us
  waiting for transfers between devices  243 us (54%)
  blocking collectives  113 us (25%)
  matrix products  50.6 us (11%)
  local copies, waits for them, and re-layouts  16 us (4%)
  between operations  13.9 us (3%)
  other arithmetic  9.62 us (2%)
    all_gather x1, waiting for transfers between devices, shards(): lax.all_gather(merged, 'fsdp', axis=0, tiled=True)  143 us
    all_gather x1, waiting for transfers between devices, shards(): lax.all_gather(w_qkv, 'fsdp', axis=0, tiled=True)  87.9 us
    pmax x1, blocking collectives, shards(): top = lax.pmax(top_part, ('dp', 'fsdp'))  62 us
    psum x1, blocking collectives, one_after_other(): partial = lax.psum(value, inner_axis)  31.6 us
    psum x1, blocking collectives, one_after_other(): return lax.psum(partial, outer_axis)  19.4 us
    dot_general x1, matrix products, shards(): jnp.dot(lax.all_gather(merged, 'fsdp', axis=0, tiled=True), w_proj, prefe...  12.5 us
    dot_general x1, matrix products, shards(): jnp.dot(columns, lax.all_gather(w_qkv, 'fsdp', axis=0, tiled=True), prefe...  12.4 us
    sub x1, matrix products, one_block(): expo = jnp.exp(scores - top)  11 us
  transfers between devices with their start and end apart: 3, of which 3 were waited for; matrix products, arithmetic and copies ran while one was open for 10% of the time, Pallas kernels for 0%

profile of v1, /device:TPU:1, one launch (start us, length us, event | category | flops | bytes accessed | tf_op | source)
XLA Modules:
  0.0 446.2 jit_solution(5782734841469964721)
XLA Ops:
  7.3 0.7 all-gather.4.cloned.1.call-update
  8.0 0.7 all-gather.6.cloned.1.call-update
  8.8 1.6 convert_reduce_fusion
  10.4 1.9 fusion.8
  12.6 87.9 %all-gather.4.cloned.1.call-done = bf16[1408,4224]{1,0:T(8,128)(2,1)} async-done(((bf16[88,4224]{1,0:T(8,128)(2,1)}), bf16[1408,4224]{1,0:T(8,128)(2,1)}) %all-gather.4.cloned.1.call-update) | async-done | bytes 11894800 | tf_op jit(solution)/shard_map/all_gather | solution.py:80
  100.5 12.4 %add_convert_fusion = bf16[512,4224]{1,0:T(8,128)(2,1)S(1)} fusion(bf16[1408,4224]{1,0:T(8,128)(2,1)} %all-gather.4.cloned.1.call-done, f32[4224]{0:T(1024)S(1)} %copy-done.7, bf16[512,1408]{1,0:T(8,128)(2,1)} %param.14, f32[1408]{0:T(1024)S(1)} %copy-done.8, f32[1408]{0:T(1024)S(1)} %copy-done.9, f32[512]{0:T(512)S(1)} %add_rsqrt_fusion.1, ...), kind=kOutput, calls=%fused_computation.5 | convolution fusion | flops 6098780160 | bytes 17694208 | tf_op jit(solution)/shard_map/dot_general | solution.py:78
  112.8 2.1 fusion.23
  115.0 2.6 copy.27
  117.6 2.5 copy.28
  120.1 2.6 copy.26
  122.7 11.0 %fusion.24 = (f32[16,512]{1,0:T(8,128)S(1)}, f32[16,512,512]{1,2,0:T(8,128)}) fusion(pred[512,512]{0,1:T(8,128)(4,1)S(1)} %compare_and_fusion, bf16[512,16,88]{0,2,1:T(8,128)(2,1)} %bitcast.17, bf16[512,16,88]{0,2,1:T(8,128)(2,1)} %bitcast.18), kind=kOutput, calls=%fused_computation.50 | convolution fusion | flops 754975232 | bytes 19955712 | tf_op jit(solution)/shard_map/while/body/eval_jaxpr/sub | solution.py:42
  133.7 8.9 %fusion.14 = bf16[16,88,512]{2,1,0:T(8,128)(2,1)} fusion(bf16[512,16,88]{0,2,1:T(8,128)(2,1)} %bitcast.19, f32[16,512,512]{1,2,0:T(8,128)} %get-tuple-element.48, f32[16,512]{1,0:T(8,128)S(1)} %get-tuple-element.47), kind=kOutput, calls=%fused_computation.26 | convolution fusion | flops 747307008 | bytes 19693568 | tf_op jit(solution)/shard_map/while/body/eval_jaxpr/hqk,khe->qhe/dot_general | solution.py:44
  142.5 10.3 %all-gather.6.cloned.1.call-done = bf16[1408,1408]{1,0:T(8,128)(2,1)} async-done(((bf16[88,1408]{1,0:T(8,128)(2,1)}), bf16[1408,1408]{1,0:T(8,128)(2,1)}) %all-gather.6.cloned.1.call-update) | async-done | bytes 3964944 | tf_op jit(solution)/shard_map/all_gather | solution.py:88
  152.9 5.9 %fusion.25 = (f32[512]{0:T(512)S(1)}, f32[512,1408]{1,0:T(8,128)S(1)}) fusion(f32[1408]{0:T(1024)S(1)} %copy-done.2, bf16[512,1408]{0,1:T(8,128)(2,1)} %bitcast.16, bf16[1408,1408]{1,0:T(8,128)(2,1)} %all-gather.6.cloned.1.call-done, bf16[512,1408]{1,0:T(8,128)(2,1)} %param.14), kind=kOutput, calls=%fused_computation.51 | convolution fusion | flops 2032926208 | bytes 9739776 | tf_op jit(solution)/shard_map/dot_general | solution.py:86
  159.5 1.7 add_convert_fusion.1
  161.2 3.6 reshape.109
  164.8 143.3 %all-gather.8.cloned.1.call-done = bf16[2048,5632]{1,0:T(8,128)(2,1)} async-done(((bf16[128,5632]{1,0:T(8,128)(2,1)}), bf16[2048,5632]{1,0:T(8,128)(2,1)}) %all-gather.8.cloned.1.call-update) | async-done | bytes 23068688 | tf_op jit(solution)/shard_map/all_gather | solution.py:96
  308.2 12.5 %fusion.22 = (f32[2048]{0:T(1024)S(1)}, f32[2048]{0:T(1024)S(1)}, f32[2048,256]{0,1:T(8,128)}) fusion(f32[256]{0:T(256)S(1)} %copy-done.10, bf16[2048,5632]{1,0:T(8,128)(2,1)} %all-gather.8.cloned.1.call-done, bf16[5632,256]{1,0:T(8,128)(2,1)S(1)} %copy-done), kind=kOutput, calls=%fused_computation.48 | convolution fusion | flops 5907673088 | bytes 28066816 | tf_op jit(solution)/shard_map/dot_general | solution.py:95
  320.9 31.6 %all-reduce = (f32[64]{0:T(128)S(1)}, f32[64]{0:T(128)S(1)}) all-reduce(f32[64]{0:T(128)S(1)} %get-tuple-element.37, f32[64]{0:T(128)S(1)} %broadcast_multiply_fusion.2), channel_id=1, replica_groups=mesh['dp'=8,'fsdp'=16] {'fsdp'}, use_global_device_ids=true, to_apply=%region_8.9 | all-reduce | flops 128 | bytes 1024 | tf_op jit(solution)/shard_map/psum | solution.py:10
  352.4 19.4 %all-reduce.1 = (f32[64]{0:T(128)S(1)}, f32[64]{0:T(128)S(1)}) all-reduce(f32[64]{0:T(128)S(1)} %get-tuple-element.38, f32[64]{0:T(128)S(1)} %get-tuple-element.39), channel_id=1, replica_groups=mesh['dp'=8,'fsdp'=16] {'dp'}, use_global_device_ids=true, to_apply=%region_9.10 | all-reduce | flops 128 | bytes 1024 | tf_op jit(solution)/shard_map/psum | solution.py:11
  372.0 62.0 %pmax.7 = f32[64]{0:T(128)S(1)} all-reduce(f32[64]{0:T(128)S(1)} %get-tuple-element.34), channel_id=1, replica_groups=mesh['dp'=8,'fsdp'=16] {'dp','fsdp'}, use_global_device_ids=true, to_apply=%region_16.17 | all-reduce | flops 64 | bytes 512 | tf_op jit(solution)/shard_map/pmax | solution.py:112
  434.0 0.5 div.47
  434.6 2.8 select_convert_fusion
  437.4 2.3 copy.30
  (38 shorter events, 1.5 us)
Async XLA Ops:
  7.2 301.0 %copy-start = (bf16[5632,256]{1,0:T(8,128)(2,1)S(1)}, bf16[5632,256]{1,0:T(8,128)(2,1)}, u32[]{:S(2)}) copy-start(bf16[5632,256]{1,0:T(8,128)(2,1)} %param.26) | copy-start | bytes 8650756
  7.2 5.1 %copy-start.6 = (s32[512]{0:T(512)S(1)}, s32[512]{0:T(512)}, u32[]{:S(2)}) copy-start(s32[512]{0:T(512)} %param.16) | copy-start | bytes 6148
  7.2 5.1 %copy-start.5 = (s32[512]{0:T(512)S(1)}, s32[512]{0:T(512)}, u32[]{:S(2)}) copy-start(s32[512]{0:T(512)} %param.15) | copy-start | bytes 6148
  7.2 93.3 %copy-start.9 = (f32[1408]{0:T(1024)S(1)}, f32[1408]{0:T(1024)}, u32[]{:S(2)}) copy-start(f32[1408]{0:T(1024)} %param.18) | copy-start | bytes 16900
  7.2 93.3 %copy-start.8 = (f32[1408]{0:T(1024)S(1)}, f32[1408]{0:T(1024)}, u32[]{:S(2)}) copy-start(f32[1408]{0:T(1024)} %param.19) | copy-start | bytes 16900
  7.2 93.3 %copy-start.7 = (f32[4224]{0:T(1024)S(1)}, f32[4224]{0:T(1024)}, u32[]{:S(2)}) copy-start(f32[4224]{0:T(1024)} %param.21) | copy-start | bytes 50692
  7.2 93.2 %all-gather.4.cloned.1.call-start = ((), (), s32[]{:S(2)}) async-start(), calls=%async_computation | async-start | bytes 12638208 | tf_op jit(solution)/shard_map/all_gather | solution.py:80
  8.0 144.9 %all-gather.6.cloned.1.call-start = ((), (), s32[]{:S(2)}) async-start(), calls=%async_computation.1 | async-start | bytes 4212736 | tf_op jit(solution)/shard_map/all_gather | solution.py:88
  8.7 299.4 %all-gather.8.cloned.1.call-start = ((), (), s32[]{:S(2)}) async-start(), calls=%async_computation.2 | async-start | bytes 24510464 | tf_op jit(solution)/shard_map/all_gather | solution.py:96
  133.7 19.2 %copy-start.2 = (f32[1408]{0:T(1024)S(1)}, f32[1408]{0:T(1024)}, u32[]{:S(2)}) copy-start(f32[1408]{0:T(1024)} %param.23) | copy-start | bytes 16900
  158.8 0.7 copy-start.3
  158.8 0.7 copy-start.4
  161.2 147.0 %copy-start.10 = (f32[256]{0:T(256)S(1)}, f32[256]{0:T(256)}, u32[]{:S(2)}) copy-start(f32[256]{0:T(256)} %param.27) | copy-start | bytes 3076
  164.8 155.8 %copy-start.1 = (s32[2048]{0:T(1024)S(1)}, s32[2048]{0:T(1024)}, u32[]{:S(2)}) copy-start(s32[2048]{0:T(1024)} %param.17) | copy-start | bytes 24580
Sparse Core Ops, SparseCore 0:
  10.2 90.2 all-gather.3
  102.6 50.2 all-gather.5
  164.9 143.1 all-gather.7
